TPU v7x, 32 devices: a whole 2x2x4 slice. The times are simulated.
32 devices in a mesh: comp: 4 (over y, core), gx: 2 (over x), gy: 4 (over z).
Axes of the slice: x: 2, y: 2, z: 4, core: 2. Of those that a mesh axis runs over, the one named last changes fastest.
Arguments:
- state: float32 [32, 32, 128, 128], P('comp', 'gx', 'gy'), may hold values from -4 to 4
- levels: int32 [32, 128], P('gx', 'gy'), may hold values from 0 to 128
- reaction: float32 [3, 8, 8], replicated, may hold values from -2 to 2
Outputs:
- new_state: float32 [32, 32, 128, 128], P('comp', 'gx', 'gy')
Inputs may be any that keep to these rules, and one draw needn't show every extreme that they name: `levels`: 0 marks a land column, 128 a column of full depth.
All inputs are finite; a program needn't handle non-finite values.
Results may differ from a plain program's by a relative error of at most 0.00018.
Values sent between devices are 32-bit elements; how exact they have to be, the bound alone decides.
No kernel may reach another device: no remote copies, remote signals or barrier semaphores. Data moves between devices by JAX's collectives and lax.ppermute only.
A program may use at most 64 MiB of HBM per device.

v0:
```python
import jax
import jax.numpy as jnp
from jax import lax
from jax.sharding import PartitionSpec as P

ITERS = 3
time_step = 0.25
lateral_mix = 0.05
vertical_mix = 0.1
pressure_scale = 0.05
thermal_coef = 1.0
haline_coef = 0.8
coriolis_mean = 0.5
coriolis_slope = 0.5


def padded_2(cells, sides, width):
    for axis, dim in sides:
        count = lax.axis_size(axis)
        head = lax.slice_in_dim(cells, 0, width, axis=dim)
        tail = lax.slice_in_dim(cells, cells.shape[dim] - width, cells.shape[dim], axis=dim)
        cells = jnp.concatenate(
            [
                lax.ppermute(tail, axis, [(i, (i + 1) % count) for i in range(count)]),
                cells,
                lax.ppermute(head, axis, [((i + 1) % count, i) for i in range(count)]),
            ],
            axis=dim,
        )
    return cells


def from_root(block, axis, source):
    block = jnp.where(lax.axis_index(axis) == source, block, jnp.zeros_like(block))
    return lax.psum(block, axis)


def along(padded, axis, shift):
    count_x = padded.shape[1] - 4
    count_y = padded.shape[2] - 4
    if axis == 1:
        return padded[:, 2 + shift : 2 + shift + count_x, 2 : 2 + count_y]
    return padded[:, 2 : 2 + count_x, 2 + shift : 2 + shift + count_y]


def centered(padded, axis):
    return (
        8.0 * (along(padded, axis, 1) - along(padded, axis, -1))
        - (along(padded, axis, 2) - along(padded, axis, -2))
    ) / 12.0


def smoothing(padded, axis):
    return (
        along(padded, axis, 2)
        + along(padded, axis, -2)
        - 4.0 * (along(padded, axis, 1) + along(padded, axis, -1))
        + 6.0 * along(padded, axis, 0)
    ) / 12.0


def transport(padded, east, north):
    return (
        east * centered(padded, 1)
        + jnp.abs(east) * smoothing(padded, 1)
        + north * centered(padded, 2)
        + jnp.abs(north) * smoothing(padded, 2)
    )


def lateral(padded):
    return (
        along(padded, 1, 1)
        + along(padded, 1, -1)
        + along(padded, 2, 1)
        + along(padded, 2, -1)
        - 4.0 * along(padded, 1, 0)
    )


def vertical(center):
    column = jnp.pad(center, ((0, 0), (0, 0), (0, 0), (1, 1)))
    return column[..., 2:] + column[..., :-2] - 2.0 * center


def dynamics_step(padded, mask, latitude, accumulate):
    center = padded[:, 2:-2, 2:-2]
    east = center[0]
    north = center[1]
    moving = padded[0:4]
    density = haline_coef * padded[3] - thermal_coef * padded[2]
    pressure = (pressure_scale * accumulate(density))[None]
    tendency = (
        lateral_mix * lateral(moving)
        + vertical_mix * vertical(center[0:4])
        - transport(moving, east, north)
    )
    rotation = (coriolis_mean + coriolis_slope * latitude)[None, :, None]
    push_east = tendency[0] + rotation * north - centered(pressure, 1)[0]
    push_north = tendency[1] - rotation * east - centered(pressure, 2)[0]
    tendency = jnp.stack([push_east, push_north, tendency[2], tendency[3]])
    advanced = center[0:4] + time_step * (1.5 * tendency - 0.5 * center[4:8])
    return jnp.concatenate([advanced * mask, tendency * mask])


def tracer_step(padded, velocity, mask, coupling):
    center = padded[:, 2:-2, 2:-2]
    growth = 2.0 * jax.nn.sigmoid(velocity[2])
    reacting = growth * jnp.einsum(
        "ij,jxyz->ixyz", coupling, center, precision=lax.Precision.HIGHEST
    )
    tendency = (
        lateral_mix * lateral(padded)
        + vertical_mix * vertical(center)
        + reacting
        - transport(padded, velocity[0], velocity[1])
    )
    return (center + time_step * tendency) * mask


def per_device(state, levels, reaction):
    cells_y = state.shape[2]
    depth_count = state.shape[3]
    slot = lax.axis_index("comp")
    row_first = lax.axis_index("gy") * cells_y
    total_rows = cells_y * lax.axis_size("gy")
    depth = lax.broadcasted_iota(jnp.int32, (1, 1, depth_count), 2)
    mask = (depth < levels[:, :, None]).astype(jnp.float32)
    lower = lax.broadcasted_iota(jnp.int32, (depth_count, depth_count), 0)
    higher = lax.broadcasted_iota(jnp.int32, (depth_count, depth_count), 1)
    summing = (lower <= higher).astype(jnp.float32)
    coupling = lax.dynamic_index_in_dim(reaction, jnp.maximum(slot - 1, 0), 0, keepdims=False)

    def accumulate(density):
        return jnp.dot(density, summing, precision=lax.Precision.HIGHEST)

    def global_rows(width):
        return row_first - width + lax.iota(jnp.int32, cells_y + 2 * width)

    def latitude(width):
        rows = global_rows(width)
        return 2.0 * rows.astype(jnp.float32) / float(total_rows - 1) - 1.0

    current = state * mask[None]
    for step in range(ITERS):
        extend_padded = padded_2(current, (("gx", 1), ("gy", 2)), 2)
        inside_rows = global_rows(2)
        region_latitude = latitude(0)

        def run_dynamics(operands):
            return dynamics_step(operands[0], operands[2], region_latitude, accumulate)

        def run_tracers(operands):
            return tracer_step(operands[0], operands[1], operands[2], coupling)

        current = lax.cond(
            slot == 0,
            run_dynamics,
            run_tracers,
            (
                extend_padded
                * ((inside_rows >= 0) & (inside_rows < total_rows)).astype(jnp.float32)[
                    None, None, :, None
                ],
                from_root(current[0:3], "comp", 0),
                mask,
            ),
        )
    return current


def solution(mesh):
    in_specs = (P("comp", "gx", "gy", None), P("gx", "gy"), P())
    out_specs = P("comp", "gx", "gy", None)
    return jax.shard_map(
        per_device, mesh=mesh, in_specs=in_specs, out_specs=out_specs, check_vma=False
    )
```

profile of v0, /device:TPU:1, one launch (start us, length us, event | category | flops | bytes accessed | tf_op | source)
XLA Modules:
  0.0 190.1 jit_solution(14269763152524657210)
XLA Ops:
  7.4 1.9 %broadcast_multiply_fusion = f32[8,16,32,128]{3,2,1,0:T(8,128)S(1)} fusion(f32[8,16,32,128]{3,2,1,0:T(8,128)} %param.9, f32[16,32,128]{2,1,0:T(8,128)S(1)} %fusion.99), kind=kLoop, calls=%fused_computation.174 | loop fusion | flops 524288 | bytes 4456448 | tf_op jit(solution)/shard_map/mul | solution.py:144
  9.4 2.1 %collective-permute-start = (f32[8,2,32,128]{3,2,1,0:T(8,128)S(1)}, f32[8,2,32,128]{3,2,1,0:T(8,128)S(1)}, u32[]{:S(2)}, u32[]{:S(2)}) collective-permute-start(f32[8,2,32,128]{3,2,1,0:T(8,128)S(1)} %get-tuple-element.149), channel_id=1, source_target_pairs={{0,4},{4,0},{1,5},{5,1},{2,6},{6,2},{3,7},{7,3},{8,12},{12,8},{9,1... | collective-permute-start | bytes 786440 | tf_op jit(solution)/shard_map/ppermute | solution.py:24
  13.2 4.2 %collective-permute-done = f32[8,2,32,128]{3,2,1,0:T(8,128)S(1)} collective-permute-done((f32[8,2,32,128]{3,2,1,0:T(8,128)S(1)}, f32[8,2,32,128]{3,2,1,0:T(8,128)S(1)}, u32[]{:S(2)}, u32[]{:S(2)}) %collective-permute-start) | collective-permute-done | bytes 262176 | tf_op jit(solution)/shard_map/ppermute | solution.py:24
  17.5 5.7 %collective-permute-done.1 = f32[8,2,32,128]{3,2,1,0:T(8,128)S(1)} collective-permute-done((f32[8,2,32,128]{3,2,1,0:T(8,128)S(1)}, f32[8,2,32,128]{3,2,1,0:T(8,128)S(1)}, u32[]{:S(2)}, u32[]{:S(2)}) %collective-permute-start.1) | collective-permute-done | bytes 262176 | tf_op jit(solution)/shard_map/ppermute | solution.py:26
  24.7 2.1 %collective-permute-start.3 = (f32[8,20,2,128]{3,2,1,0:T(2,128)S(1)}, f32[8,20,2,128]{3,2,1,0:T(2,128)}, u32[]{:S(2)}, u32[]{:S(2)}) collective-permute-start(f32[8,20,2,128]{3,2,1,0:T(2,128)S(1)} %get-tuple-element.144), channel_id=1, source_target_pairs={{1,0},{2,1},{3,2},{0,3},{5,4},{6,5},{7,6},{4,7},{9,8},{10,9},{11,1... | collective-permute-start | bytes 491528 | tf_op jit(solution)/shard_map/ppermute | solution.py:26
  26.8 3.1 %collective-permute-done.2 = f32[8,20,2,128]{3,2,1,0:T(2,128)S(1)} collective-permute-done((f32[8,20,2,128]{3,2,1,0:T(2,128)S(1)}, f32[8,20,2,128]{3,2,1,0:T(2,128)S(1)}, u32[]{:S(2)}, u32[]{:S(2)}) %collective-permute-start.2) | collective-permute-done | bytes 163872 | tf_op jit(solution)/shard_map/ppermute | solution.py:24
  30.5 3.3 %collective-permute-done.3 = f32[8,20,2,128]{3,2,1,0:T(2,128)} collective-permute-done((f32[8,20,2,128]{3,2,1,0:T(2,128)S(1)}, f32[8,20,2,128]{3,2,1,0:T(2,128)}, u32[]{:S(2)}, u32[]{:S(2)}) %collective-permute-start.3) | collective-permute-done | bytes 163872 | tf_op jit(solution)/shard_map/ppermute | solution.py:26
  33.8 2.3 %maximum_multiply_fusion = f32[8,20,36,128]{3,2,1,0:T(8,128)S(1)} fusion(f32[8,20,2,128]{3,2,1,0:T(2,128)} %collective-permute-done.3, f32[8,2,32,128]{3,2,1,0:T(8,128)} %copy-done.7, f32[8,16,32,128]{3,2,1,0:T(8,128)} %copy-done.2, f32[8,2,32,128]{3,2,1,0:T(8,128)} %copy-done.6, f32[8,20,2,128]{3,2,1,0:T(2,128)} %copy-done.14, f32[36]{0:T(128)S(1)} %and_convert_fusion), kind=kLoop, calls=%fused_computation.171 | loop fusion | flops 3686400 | bytes 5898384 | tf_op jit(solution)/shard_map/mul | solution.py:161
  36.1 12.0 %all-reduce.10.cloned.1.call-done = f32[3,16,32,128]{3,2,1,0:T(8,128)} async-done(((f32[3,16,32,128]{3,2,1,0:T(8,128)}), f32[3,16,32,128]{3,2,1,0:T(8,128)}) %all-reduce.10.cloned.1.call-update) | async-done | bytes 786448 | tf_op jit(solution)/shard_map/psum | solution.py:35
  48.1 9.7 %conditional.3 = (f32[8,16,32,128]{3,2,1,0:T(8,128)S(1)}) conditional(s32[]{:T(128)} %convert_element_type.41, (f32[8,20,36,128]{3,2,1,0:T(8,128)S(1)}, f32[3,16,32,128]{3,2,1,0:T(8,128)}, f32[8,8]{1,0:T(8,128)S(1)}, f32[16,32,128]{2,1,0:T(8,128)S(1)}) %tuple.23, (f32[8,20,36,128]{3,2,1,0:T(8,128)S(1)}, f32[32]{0:T(128)S(1)}, f32[128,128]{1,0:T(8,128)}, ...), branch_computations={%region_1.2_spmd, %region_2.3_spmd} | conditional | flops 155859008 | bytes 41029640 | solution.py:156
  49.4 1.7 copy.9
  51.2 6.1 %fusion.8 = f32[8,16,32,128]{3,0,2,1:T(8,128)S(1)} fusion(f32[8,16,32,128]{3,0,2,1:T(8,128)S(1)} %slice.573, f32[8,20,36,128]{3,0,2,1:T(8,128)S(1)} %copy.9, f32[16,32,128]{2,1,0:T(8,128)S(1)} %get-tuple-element.65, f32[16,32,128]{2,1,0:T(8,128)S(1)} %get-tuple-element.102, f32[16,32,128]{2,1,0:T(8,128)S(1)} %get-tuple-element.104, ...), kind=kOutput, calls=%fused_computation.10 | convolution fusion | flops 72351744 | bytes 24645632 | tf_op jit(solution)/shard_map/cond/branch_0_fun/ij,jxyz->ixyz/dot_general | solution.py:109
  57.9 1.7 collective-permute-start.4
  59.6 6.8 %collective-permute-done.4 = f32[8,2,32,128]{3,2,1,0:T(8,128)S(1)} collective-permute-done((f32[8,2,32,128]{3,2,1,0:T(8,128)S(1)}, f32[8,2,32,128]{3,2,1,0:T(8,128)S(1)}, u32[]{:S(2)}, u32[]{:S(2)}) %collective-permute-start.4) | collective-permute-done | bytes 262176 | tf_op jit(solution)/shard_map/ppermute | solution.py:24
  66.4 2.8 %collective-permute-done.5 = f32[8,2,32,128]{3,2,1,0:T(8,128)S(1)} collective-permute-done((f32[8,2,32,128]{3,2,1,0:T(8,128)S(1)}, f32[8,2,32,128]{3,2,1,0:T(8,128)S(1)}, u32[]{:S(2)}, u32[]{:S(2)}) %collective-permute-start.5) | collective-permute-done | bytes 262176 | tf_op jit(solution)/shard_map/ppermute | solution.py:26
  71.1 2.1 %collective-permute-start.7 = (f32[8,20,2,128]{3,2,1,0:T(2,128)S(1)}, f32[8,20,2,128]{3,2,1,0:T(2,128)}, u32[]{:S(2)}, u32[]{:S(2)}) collective-permute-start(f32[8,20,2,128]{3,2,1,0:T(2,128)S(1)} %get-tuple-element.142), channel_id=1, source_target_pairs={{1,0},{2,1},{3,2},{0,3},{5,4},{6,5},{7,6},{4,7},{9,8},{10,9},{11,1... | collective-permute-start | bytes 491528 | tf_op jit(solution)/shard_map/ppermute | solution.py:26
  74.2 3.5 %collective-permute-done.6 = f32[8,20,2,128]{3,2,1,0:T(2,128)S(1)} collective-permute-done((f32[8,20,2,128]{3,2,1,0:T(2,128)S(1)}, f32[8,20,2,128]{3,2,1,0:T(2,128)S(1)}, u32[]{:S(2)}, u32[]{:S(2)}) %collective-permute-start.6) | collective-permute-done | bytes 163872 | tf_op jit(solution)/shard_map/ppermute | solution.py:24
  79.3 2.3 %maximum_multiply_fusion.1 = f32[8,20,36,128]{3,2,1,0:T(8,128)S(1)} fusion(f32[8,20,2,128]{3,2,1,0:T(2,128)} %collective-permute-done.7, f32[8,2,32,128]{3,2,1,0:T(8,128)} %copy-done.10, f32[8,16,32,128]{3,2,1,0:T(8,128)} %copy-done.3, f32[8,2,32,128]{3,2,1,0:T(8,128)} %copy-done.8, f32[8,20,2,128]{3,2,1,0:T(2,128)} %copy-done.12, f32[36]{0:T(128)S(1)} %and_convert_fusion), kind=kLoop, calls=%fused_computation.172 | loop fusion | flops 3686400 | bytes 5898384 | tf_op jit(solution)/shard_map/mul | solution.py:161
  81.5 28.3 %all-reduce.12.cloned.1.call-done = f32[3,16,32,128]{3,2,1,0:T(8,128)} async-done(((f32[3,16,32,128]{3,2,1,0:T(8,128)}), f32[3,16,32,128]{3,2,1,0:T(8,128)}) %all-reduce.12.cloned.1.call-update) | async-done | bytes 786448 | tf_op jit(solution)/shard_map/psum | solution.py:35
  109.8 9.7 %conditional.4 = (f32[8,16,32,128]{3,2,1,0:T(8,128)S(1)}) conditional(s32[]{:T(128)} %convert_element_type.41, (f32[8,20,36,128]{3,2,1,0:T(8,128)S(1)}, f32[3,16,32,128]{3,2,1,0:T(8,128)}, f32[8,8]{1,0:T(8,128)S(1)}, f32[16,32,128]{2,1,0:T(8,128)S(1)}) %tuple.25, (f32[8,20,36,128]{3,2,1,0:T(8,128)S(1)}, f32[32]{0:T(128)S(1)}, f32[128,128]{1,0:T(8,128)}, ...), branch_computations={%region_4.5_spmd, %region_5.6_spmd} | conditional | flops 155859008 | bytes 41029640 | solution.py:156
  111.1 1.7 copy.10
  113.0 6.1 %fusion.41 = f32[8,16,32,128]{3,0,2,1:T(8,128)S(1)} fusion(f32[8,16,32,128]{3,0,2,1:T(8,128)S(1)} %slice.593, f32[8,20,36,128]{3,0,2,1:T(8,128)S(1)} %copy.10, f32[16,32,128]{2,1,0:T(8,128)S(1)} %get-tuple-element.73, f32[16,32,128]{2,1,0:T(8,128)S(1)} %get-tuple-element.115, f32[16,32,128]{2,1,0:T(8,128)S(1)} %get-tuple-element.117, ...), kind=kOutput, calls=%fused_computation.67 | convolution fusion | flops 72351744 | bytes 24645632 | tf_op jit(solution)/shard_map/cond/branch_0_fun/ij,jxyz->ixyz/dot_general | solution.py:109
  119.6 1.7 collective-permute-start.8
  121.4 6.8 %collective-permute-done.8 = f32[8,2,32,128]{3,2,1,0:T(8,128)S(1)} collective-permute-done((f32[8,2,32,128]{3,2,1,0:T(8,128)S(1)}, f32[8,2,32,128]{3,2,1,0:T(8,128)S(1)}, u32[]{:S(2)}, u32[]{:S(2)}) %collective-permute-start.8) | collective-permute-done | bytes 262176 | tf_op jit(solution)/shard_map/ppermute | solution.py:24
  128.2 2.8 %collective-permute-done.9 = f32[8,2,32,128]{3,2,1,0:T(8,128)S(1)} collective-permute-done((f32[8,2,32,128]{3,2,1,0:T(8,128)S(1)}, f32[8,2,32,128]{3,2,1,0:T(8,128)S(1)}, u32[]{:S(2)}, u32[]{:S(2)}) %collective-permute-start.9) | collective-permute-done | bytes 262176 | tf_op jit(solution)/shard_map/ppermute | solution.py:26
  132.9 2.1 %collective-permute-start.11 = (f32[8,20,2,128]{3,2,1,0:T(2,128)S(1)}, f32[8,20,2,128]{3,2,1,0:T(2,128)}, u32[]{:S(2)}, u32[]{:S(2)}) collective-permute-start(f32[8,20,2,128]{3,2,1,0:T(2,128)S(1)} %get-tuple-element.140), channel_id=1, source_target_pairs={{1,0},{2,1},{3,2},{0,3},{5,4},{6,5},{7,6},{4,7},{9,8},{10,9},{11,1... | collective-permute-start | bytes 491528 | tf_op jit(solution)/shard_map/ppermute | solution.py:26
  135.9 3.5 %collective-permute-done.10 = f32[8,20,2,128]{3,2,1,0:T(2,128)S(1)} collective-permute-done((f32[8,20,2,128]{3,2,1,0:T(2,128)S(1)}, f32[8,20,2,128]{3,2,1,0:T(2,128)S(1)}, u32[]{:S(2)}, u32[]{:S(2)}) %collective-permute-start.10) | collective-permute-done | bytes 163872 | tf_op jit(solution)/shard_map/ppermute | solution.py:24
  141.0 2.3 %maximum_multiply_fusion.2 = f32[8,20,36,128]{3,2,1,0:T(8,128)S(1)} fusion(f32[8,20,2,128]{3,2,1,0:T(2,128)} %collective-permute-done.11, f32[8,2,32,128]{3,2,1,0:T(8,128)} %copy-done.11, f32[8,16,32,128]{3,2,1,0:T(8,128)} %copy-done.4, f32[8,2,32,128]{3,2,1,0:T(8,128)} %copy-done.9, f32[8,20,2,128]{3,2,1,0:T(2,128)} %copy-done.13, f32[36]{0:T(128)S(1)} %and_convert_fusion), kind=kLoop, calls=%fused_computation.173 | loop fusion | flops 3686400 | bytes 5898384 | tf_op jit(solution)/shard_map/mul | solution.py:161
  143.3 28.3 %all-reduce.14.cloned.1.call-done = f32[3,16,32,128]{3,2,1,0:T(8,128)} async-done(((f32[3,16,32,128]{3,2,1,0:T(8,128)}), f32[3,16,32,128]{3,2,1,0:T(8,128)}) %all-reduce.14.cloned.1.call-update) | async-done | bytes 786448 | tf_op jit(solution)/shard_map/psum | solution.py:35
  171.6 9.9 %conditional.5 = (f32[8,16,32,128]{3,2,1,0:T(8,128)S(1)}) conditional(s32[]{:T(128)} %convert_element_type.41, (f32[8,20,36,128]{3,2,1,0:T(8,128)S(1)}, f32[3,16,32,128]{3,2,1,0:T(8,128)}, f32[8,8]{1,0:T(8,128)S(1)}, f32[16,32,128]{2,1,0:T(8,128)S(1)}) %tuple.27, (f32[8,20,36,128]{3,2,1,0:T(8,128)S(1)}, f32[32]{0:T(128)S(1)}, f32[128,128]{1,0:T(8,128)}, ...), branch_computations={%region_7.8_spmd, %region_8.9_spmd} | conditional | flops 155859008 | bytes 41029640 | solution.py:156
  172.9 1.7 copy.11
  174.8 6.1 %fusion.74 = f32[8,16,32,128]{3,0,2,1:T(8,128)S(1)} fusion(f32[8,16,32,128]{3,0,2,1:T(8,128)S(1)} %slice.613, f32[8,20,36,128]{3,0,2,1:T(8,128)S(1)} %copy.11, f32[16,32,128]{2,1,0:T(8,128)S(1)} %get-tuple-element.81, f32[16,32,128]{2,1,0:T(8,128)S(1)} %get-tuple-element.128, f32[16,32,128]{2,1,0:T(8,128)S(1)} %get-tuple-element.130, ...), kind=kOutput, calls=%fused_computation.124 | convolution fusion | flops 72351744 | bytes 24645632 | tf_op jit(solution)/shard_map/cond/branch_0_fun/ij,jxyz->ixyz/dot_general | solution.py:109
  (67 shorter events, 21.5 us)
Async XLA Ops:
  6.5 6.1 %copy-start = (f32[3,8,8]{2,1,0:T(8,128)S(1)}, f32[3,8,8]{2,1,0:T(8,128)}, u32[]{:S(2)}) copy-start(f32[3,8,8]{2,1,0:T(8,128)} %param.11) | copy-start | bytes 2308
  6.5 41.6 %all-reduce.10.cloned.1.call-start = ((), (), s32[]{:S(2)}) async-start(), calls=%async_computation | async-start | bytes 1572864 | tf_op jit(solution)/shard_map/psum | solution.py:35
  9.3 14.0 %copy-start.2 = (f32[8,16,32,128]{3,2,1,0:T(8,128)}, f32[8,16,32,128]{3,2,1,0:T(8,128)S(1)}, u32[]{:S(2)}) copy-start(f32[8,16,32,128]{3,2,1,0:T(8,128)S(1)} %broadcast_multiply_fusion) | copy-start | bytes 6291460
  9.4 8.1 %collective-permute-start = (f32[8,2,32,128]{3,2,1,0:T(8,128)S(1)}, f32[8,2,32,128]{3,2,1,0:T(8,128)S(1)}, u32[]{:S(2)}, u32[]{:S(2)}) collective-permute-start(f32[8,2,32,128]{3,2,1,0:T(8,128)S(1)} %get-tuple-element.149), channel_id=1, source_target_pairs={{0,4},{4,0},{1,5},{5,1},{2,6},{6,2},{3,7},{7,3},{8,12},{12,8},{9,1... | collective-permute-start | bytes 786440 | tf_op jit(solution)/shard_map/ppermute | solution.py:24
  11.5 11.7 %collective-permute-start.1 = (f32[8,2,32,128]{3,2,1,0:T(8,128)S(1)}, f32[8,2,32,128]{3,2,1,0:T(8,128)S(1)}, u32[]{:S(2)}, u32[]{:S(2)}) collective-permute-start(f32[8,2,32,128]{3,2,1,0:T(8,128)S(1)} %get-tuple-element.150), channel_id=1, source_target_pairs={{4,0},{0,4},{5,1},{1,5},{6,2},{2,6},{7,3},{3,7},{12,8},{8,12},{13,... | collective-permute-start | bytes 786440 | tf_op jit(solution)/shard_map/ppermute | solution.py:26
  12.5 97.3 %all-reduce.12.cloned.1.call-start = ((), (), s32[]{:S(2)}) async-start(), calls=%async_computation.1 | async-start | bytes 1572864 | tf_op jit(solution)/shard_map/psum | solution.py:35
  17.5 12.4 %copy-start.6 = (f32[8,2,32,128]{3,2,1,0:T(8,128)}, f32[8,2,32,128]{3,2,1,0:T(8,128)S(1)}, u32[]{:S(2)}) copy-start(f32[8,2,32,128]{3,2,1,0:T(8,128)S(1)} %collective-permute-done) | copy-start | bytes 786436
  23.2 6.6 %copy-start.7 = (f32[8,2,32,128]{3,2,1,0:T(8,128)}, f32[8,2,32,128]{3,2,1,0:T(8,128)S(1)}, u32[]{:S(2)}) copy-start(f32[8,2,32,128]{3,2,1,0:T(8,128)S(1)} %collective-permute-done.1) | copy-start | bytes 786436
  23.3 6.5 %collective-permute-start.2 = (f32[8,20,2,128]{3,2,1,0:T(2,128)S(1)}, f32[8,20,2,128]{3,2,1,0:T(2,128)S(1)}, u32[]{:S(2)}, u32[]{:S(2)}) collective-permute-start(f32[8,20,2,128]{3,2,1,0:T(2,128)S(1)} %get-tuple-element.143), channel_id=1, source_target_pairs={{0,1},{1,2},{2,3},{3,0},{4,5},{5,6},{6,7},{7,4},{8,9},{9,10},{10,1... | collective-permute-start | bytes 491528 | tf_op jit(solution)/shard_map/ppermute | solution.py:24
  24.7 9.2 %collective-permute-start.3 = (f32[8,20,2,128]{3,2,1,0:T(2,128)S(1)}, f32[8,20,2,128]{3,2,1,0:T(2,128)}, u32[]{:S(2)}, u32[]{:S(2)}) collective-permute-start(f32[8,20,2,128]{3,2,1,0:T(2,128)S(1)} %get-tuple-element.144), channel_id=1, source_target_pairs={{1,0},{2,1},{3,2},{0,3},{5,4},{6,5},{7,6},{4,7},{9,8},{10,9},{11,1... | collective-permute-start | bytes 491528 | tf_op jit(solution)/shard_map/ppermute | solution.py:26
  29.8 0.7 copy-start.14
  57.8 16.3 %copy-start.3 = (f32[8,16,32,128]{3,2,1,0:T(8,128)}, f32[8,16,32,128]{3,2,1,0:T(8,128)S(1)}, u32[]{:S(2)}) copy-start(f32[8,16,32,128]{3,2,1,0:T(8,128)S(1)} %get-tuple-element.153) | copy-start | bytes 6291460
  57.9 8.5 %collective-permute-start.4 = (f32[8,2,32,128]{3,2,1,0:T(8,128)S(1)}, f32[8,2,32,128]{3,2,1,0:T(8,128)S(1)}, u32[]{:S(2)}, u32[]{:S(2)}) collective-permute-start(f32[8,2,32,128]{3,2,1,0:T(8,128)S(1)} %get-tuple-element.147), channel_id=1, source_target_pairs={{0,4},{4,0},{1,5},{5,1},{2,6},{6,2},{3,7},{7,3},{8,12},{12,8},{9,1... | collective-permute-start | bytes 786440 | tf_op jit(solution)/shard_map/ppermute | solution.py:24
  59.5 9.6 %collective-permute-start.5 = (f32[8,2,32,128]{3,2,1,0:T(8,128)S(1)}, f32[8,2,32,128]{3,2,1,0:T(8,128)S(1)}, u32[]{:S(2)}, u32[]{:S(2)}) collective-permute-start(f32[8,2,32,128]{3,2,1,0:T(8,128)S(1)} %get-tuple-element.148), channel_id=1, source_target_pairs={{4,0},{0,4},{5,1},{1,5},{6,2},{2,6},{7,3},{3,7},{12,8},{8,12},{13,... | collective-permute-start | bytes 786440 | tf_op jit(solution)/shard_map/ppermute | solution.py:26
  66.4 2.8 %copy-start.8 = (f32[8,2,32,128]{3,2,1,0:T(8,128)}, f32[8,2,32,128]{3,2,1,0:T(8,128)S(1)}, u32[]{:S(2)}) copy-start(f32[8,2,32,128]{3,2,1,0:T(8,128)S(1)} %collective-permute-done.4) | copy-start | bytes 786436
  69.2 0.7 copy-start.10
  69.9 7.8 %collective-permute-start.6 = (f32[8,20,2,128]{3,2,1,0:T(2,128)S(1)}, f32[8,20,2,128]{3,2,1,0:T(2,128)S(1)}, u32[]{:S(2)}, u32[]{:S(2)}) collective-permute-start(f32[8,20,2,128]{3,2,1,0:T(2,128)S(1)} %get-tuple-element.141), channel_id=1, source_target_pairs={{0,1},{1,2},{2,3},{3,0},{4,5},{5,6},{6,7},{7,4},{8,9},{9,10},{10,1... | collective-permute-start | bytes 491528 | tf_op jit(solution)/shard_map/ppermute | solution.py:24
  71.1 8.2 %collective-permute-start.7 = (f32[8,20,2,128]{3,2,1,0:T(2,128)S(1)}, f32[8,20,2,128]{3,2,1,0:T(2,128)}, u32[]{:S(2)}, u32[]{:S(2)}) collective-permute-start(f32[8,20,2,128]{3,2,1,0:T(2,128)S(1)} %get-tuple-element.142), channel_id=1, source_target_pairs={{1,0},{2,1},{3,2},{0,3},{5,4},{6,5},{7,6},{4,7},{9,8},{10,9},{11,1... | collective-permute-start | bytes 491528 | tf_op jit(solution)/shard_map/ppermute | solution.py:26
  74.2 97.4 %all-reduce.14.cloned.1.call-start = ((), (), s32[]{:S(2)}) async-start(), calls=%async_computation.2 | async-start | bytes 1572864 | tf_op jit(solution)/shard_map/psum | solution.py:35
  77.7 0.7 copy-start.12
  119.6 16.3 %copy-start.4 = (f32[8,16,32,128]{3,2,1,0:T(8,128)}, f32[8,16,32,128]{3,2,1,0:T(8,128)S(1)}, u32[]{:S(2)}) copy-start(f32[8,16,32,128]{3,2,1,0:T(8,128)S(1)} %get-tuple-element.154) | copy-start | bytes 6291460
  119.6 8.5 %collective-permute-start.8 = (f32[8,2,32,128]{3,2,1,0:T(8,128)S(1)}, f32[8,2,32,128]{3,2,1,0:T(8,128)S(1)}, u32[]{:S(2)}, u32[]{:S(2)}) collective-permute-start(f32[8,2,32,128]{3,2,1,0:T(8,128)S(1)} %get-tuple-element.145), channel_id=1, source_target_pairs={{0,4},{4,0},{1,5},{5,1},{2,6},{6,2},{3,7},{7,3},{8,12},{12,8},{9,1... | collective-permute-start | bytes 786440 | tf_op jit(solution)/shard_map/ppermute | solution.py:24
  121.3 9.6 %collective-permute-start.9 = (f32[8,2,32,128]{3,2,1,0:T(8,128)S(1)}, f32[8,2,32,128]{3,2,1,0:T(8,128)S(1)}, u32[]{:S(2)}, u32[]{:S(2)}) collective-permute-start(f32[8,2,32,128]{3,2,1,0:T(8,128)S(1)} %get-tuple-element.146), channel_id=1, source_target_pairs={{4,0},{0,4},{5,1},{1,5},{6,2},{2,6},{7,3},{3,7},{12,8},{8,12},{13,... | collective-permute-start | bytes 786440 | tf_op jit(solution)/shard_map/ppermute | solution.py:26
  128.2 2.8 %copy-start.9 = (f32[8,2,32,128]{3,2,1,0:T(8,128)}, f32[8,2,32,128]{3,2,1,0:T(8,128)S(1)}, u32[]{:S(2)}) copy-start(f32[8,2,32,128]{3,2,1,0:T(8,128)S(1)} %collective-permute-done.8) | copy-start | bytes 786436
  130.9 0.7 copy-start.11
  131.7 7.8 %collective-permute-start.10 = (f32[8,20,2,128]{3,2,1,0:T(2,128)S(1)}, f32[8,20,2,128]{3,2,1,0:T(2,128)S(1)}, u32[]{:S(2)}, u32[]{:S(2)}) collective-permute-start(f32[8,20,2,128]{3,2,1,0:T(2,128)S(1)} %get-tuple-element.139), channel_id=1, source_target_pairs={{0,1},{1,2},{2,3},{3,0},{4,5},{5,6},{6,7},{7,4},{8,9},{9,10},{10,1... | collective-permute-start | bytes 491528 | tf_op jit(solution)/shard_map/ppermute | solution.py:24
  132.9 8.2 %collective-permute-start.11 = (f32[8,20,2,128]{3,2,1,0:T(2,128)S(1)}, f32[8,20,2,128]{3,2,1,0:T(2,128)}, u32[]{:S(2)}, u32[]{:S(2)}) collective-permute-start(f32[8,20,2,128]{3,2,1,0:T(2,128)S(1)} %get-tuple-element.140), channel_id=1, source_target_pairs={{1,0},{2,1},{3,2},{0,3},{5,4},{6,5},{7,6},{4,7},{9,8},{10,9},{11,1... | collective-permute-start | bytes 491528 | tf_op jit(solution)/shard_map/ppermute | solution.py:26
  139.4 0.7 copy-start.13
  181.5 1.3 copy-start.5
  182.9 0.7 copy-start.1
Sparse Core Ops, SparseCore 0:
  12.7 35.3 all-reduce.9
  74.3 35.5 all-reduce.11
  136.0 35.5 all-reduce.13
where the time goes:
time: 191 us; the launch traced here: 190 us
  waiting for transfers between devices  113 us (59%)
  matrix products  18.4 us (10%)
  other arithmetic  17.3 us (9%)
  starting transfers between devices  15.7 us (8%)
  between operations  13.3 us (7%)
  local copies, waits for them, and re-layouts  12.1 us (6%)
    psum x3, waiting for transfers between devices, from_root(): return lax.psum(block, axis)  68.6 us
    ppermute x6, waiting for transfers between devices, padded_2(): lax.ppermute(tail, axis, [(i, (i + 1) % count) for i in range(count)])  27.8 us
    dot_general x3, matrix products, tracer_step(): jnp.einsum('ij,jxyz->ixyz', coupling, center, precision=lax.Precision.HIG...  18.4 us
    ppermute x6, waiting for transfers between devices, padded_2(): lax.ppermute(head, axis, [((i + 1) % count, i) for i in range(count)])  16.5 us
    ppermute x6, starting transfers between devices, padded_2(): lax.ppermute(tail, axis, [(i, (i + 1) % count) for i in range(count)])  9.18 us
    mul x3, other arithmetic, per_device(): extend_padded * ((inside_rows >= 0) & (inside_rows < total_rows)).astype(...  6.8 us
    ppermute x6, starting transfers between devices, padded_2(): lax.ppermute(head, axis, [((i + 1) % count, i) for i in range(count)])  6.44 us
    unnamed x30, local copies, waits for them, and re-layouts  5.23 us
  transfers between devices with their start and end apart: 15, of which 15 were waited for; matrix products, arithmetic and copies ran while one was open for 5% of the time, Pallas kernels for 0%

commit v1 on v0

--- a/solution.py
+++ b/solution.py
@@ -32,7 +32,7 @@
 
 def from_root(block, axis, source):
     block = jnp.where(lax.axis_index(axis) == source, block, jnp.zeros_like(block))
-    return lax.psum(block, axis)
+    return jnp.sum(lax.all_gather(block, axis), axis=0)
 
 
 def along(padded, axis, shift):

time: 191 us -> 149 us (0.78)
  waiting for transfers between devices: 113 us -> 64.1 us
  other arithmetic: 17.3 us -> 27.4 us
  local copies, waits for them, and re-layouts: 12.1 us -> 9.62 us
    psum x3 -> x0, waiting for transfers between devices: 68.6 us -> none  [from_root(): return lax.psum(block, axis)]
    all_gather x0 -> x3, waiting for transfers between devices: none -> 25 us  [from_root(): return jnp.sum(lax.all_gather(block, axis), axis=0)]
    reduce_sum x0 -> x3, other arithmetic: none -> 9.59 us  [from_root(): return jnp.sum(lax.all_gather(block, axis), axis=0)]
    ppermute x6, waiting for transfers between devices: 27.8 us -> 21 us  [padded_2(): lax.ppermute(tail, axis, [(i, (i + 1) % count) for i in range(count)])]
    unnamed x30 -> x20, local copies, waits for them, and re-layouts: 5.23 us -> 2.72 us
  transfers between devices with their start and end apart: 15 -> 15, of which waited for: 15 -> 15; matrix products, arithmetic and copies ran while one was open for 5% -> 6% of each run, Pallas kernels for 0% -> 0%
where the time goes in v1:
time: 149 us; the launch traced here: 148 us
  waiting for transfers between devices  64.1 us (43%)
  other arithmetic  27.4 us (18%)
  matrix products  18.4 us (12%)
  starting transfers between devices  15.4 us (10%)
  between operations  13.3 us (9%)
  local copies, waits for them, and re-layouts  9.62 us (6%)
    all_gather x3, waiting for transfers between devices, from_root(): return jnp.sum(lax.all_gather(block, axis), axis=0)  25 us
    ppermute x6, waiting for transfers between devices, padded_2(): lax.ppermute(tail, axis, [(i, (i + 1) % count) for i in range(count)])  21 us
    dot_general x3, matrix products, tracer_step(): jnp.einsum('ij,jxyz->ixyz', coupling, center, precision=lax.Precision.HIG...  18.4 us
    ppermute x6, waiting for transfers between devices, padded_2(): lax.ppermute(head, axis, [((i + 1) % count, i) for i in range(count)])  18.2 us
    reduce_sum x3, other arithmetic, from_root(): return jnp.sum(lax.all_gather(block, axis), axis=0)  9.59 us
    ppermute x6, starting transfers between devices, padded_2(): lax.ppermute(tail, axis, [(i, (i + 1) % count) for i in range(count)])  8.43 us
    ppermute x6, starting transfers between devices, padded_2(): lax.ppermute(head, axis, [((i + 1) % count, i) for i in range(count)])  6.84 us
    mul x3, other arithmetic, per_device(): extend_padded * ((inside_rows >= 0) & (inside_rows < total_rows)).astype(...  6.57 us
  transfers between devices with their start and end apart: 15, of which 15 were waited for; matrix products, arithmetic and copies ran while one was open for 6% of the time, Pallas kernels for 0%

profile of v1, /device:TPU:1, one launch (start us, length us, event | category | flops | bytes accessed | tf_op | source)
XLA Modules:
  0.0 148.5 jit_solution(1359476267366360716)
XLA Ops:
  7.4 1.9 %broadcast_multiply_fusion = f32[8,16,32,128]{3,2,1,0:T(8,128)S(1)} fusion(f32[8,16,32,128]{3,2,1,0:T(8,128)} %param.9, f32[16,32,128]{2,1,0:T(8,128)S(1)} %fusion.114), kind=kLoop, calls=%fused_computation.189 | loop fusion | flops 524288 | bytes 4456448 | tf_op jit(solution)/shard_map/mul | solution.py:144
  10.5 2.1 %collective-permute-start = (f32[8,2,32,128]{3,2,1,0:T(8,128)S(1)}, f32[8,2,32,128]{3,2,1,0:T(8,128)S(1)}, u32[]{:S(2)}, u32[]{:S(2)}) collective-permute-start(f32[8,2,32,128]{3,2,1,0:T(8,128)S(1)} %get-tuple-element.168), channel_id=1, source_target_pairs={{0,4},{4,0},{1,5},{5,1},{2,6},{6,2},{3,7},{7,3},{8,12},{12,8},{9,1... | collective-permute-start | bytes 786440 | tf_op jit(solution)/shard_map/ppermute | solution.py:24
  13.2 5.4 %collective-permute-done = f32[8,2,32,128]{3,2,1,0:T(8,128)S(1)} collective-permute-done((f32[8,2,32,128]{3,2,1,0:T(8,128)S(1)}, f32[8,2,32,128]{3,2,1,0:T(8,128)S(1)}, u32[]{:S(2)}, u32[]{:S(2)}) %collective-permute-start) | collective-permute-done | bytes 262176 | tf_op jit(solution)/shard_map/ppermute | solution.py:24
  18.6 5.7 %collective-permute-done.1 = f32[8,2,32,128]{3,2,1,0:T(8,128)S(1)} collective-permute-done((f32[8,2,32,128]{3,2,1,0:T(8,128)S(1)}, f32[8,2,32,128]{3,2,1,0:T(8,128)S(1)}, u32[]{:S(2)}, u32[]{:S(2)}) %collective-permute-start.1) | collective-permute-done | bytes 262176 | tf_op jit(solution)/shard_map/ppermute | solution.py:26
  25.8 2.1 %collective-permute-start.3 = (f32[8,20,2,128]{3,2,1,0:T(2,128)S(1)}, f32[8,20,2,128]{3,2,1,0:T(2,128)}, u32[]{:S(2)}, u32[]{:S(2)}) collective-permute-start(f32[8,20,2,128]{3,2,1,0:T(2,128)S(1)} %get-tuple-element.163), channel_id=1, source_target_pairs={{1,0},{2,1},{3,2},{0,3},{5,4},{6,5},{7,6},{4,7},{9,8},{10,9},{11,1... | collective-permute-start | bytes 491528 | tf_op jit(solution)/shard_map/ppermute | solution.py:26
  28.5 2.4 %collective-permute-done.2 = f32[8,20,2,128]{3,2,1,0:T(2,128)S(1)} collective-permute-done((f32[8,20,2,128]{3,2,1,0:T(2,128)S(1)}, f32[8,20,2,128]{3,2,1,0:T(2,128)S(1)}, u32[]{:S(2)}, u32[]{:S(2)}) %collective-permute-start.2) | collective-permute-done | bytes 163872 | tf_op jit(solution)/shard_map/ppermute | solution.py:24
  31.6 3.3 %collective-permute-done.3 = f32[8,20,2,128]{3,2,1,0:T(2,128)} collective-permute-done((f32[8,20,2,128]{3,2,1,0:T(2,128)S(1)}, f32[8,20,2,128]{3,2,1,0:T(2,128)}, u32[]{:S(2)}, u32[]{:S(2)}) %collective-permute-start.3) | collective-permute-done | bytes 163872 | tf_op jit(solution)/shard_map/ppermute | solution.py:26
  34.9 2.3 %maximum_multiply_fusion = f32[8,20,36,128]{3,2,1,0:T(8,128)S(1)} fusion(f32[8,20,2,128]{3,2,1,0:T(2,128)} %collective-permute-done.3, f32[8,2,32,128]{3,2,1,0:T(8,128)} %copy-done.7, f32[8,16,32,128]{3,2,1,0:T(8,128)} %copy-done.2, f32[8,2,32,128]{3,2,1,0:T(8,128)} %copy-done.6, f32[8,20,2,128]{3,2,1,0:T(2,128)} %copy-done.8, f32[36]{0:T(128)S(1)} %and_convert_fusion), kind=kLoop, calls=%fused_computation.186 | loop fusion | flops 3686400 | bytes 5898384 | tf_op jit(solution)/shard_map/mul | solution.py:161
  37.2 4.3 %all-gather.7.cloned.1.call-done = f32[12,16,32,128]{3,2,1,0:T(8,128)} async-done(((f32[3,16,32,128]{3,2,1,0:T(8,128)}), f32[12,16,32,128]{3,2,1,0:T(8,128)}) %all-gather.7.cloned.1.call-update) | async-done | bytes 3145744 | tf_op jit(solution)/shard_map/all_gather | solution.py:35
  41.5 12.9 %conditional.3 = (f32[8,16,32,128]{3,2,1,0:T(8,128)S(1)}) conditional(s32[]{:T(128)} %convert_element_type.41, (f32[8,20,36,128]{3,2,1,0:T(8,128)S(1)}, f32[4,3,16,32,128]{4,3,2,1,0:T(8,128)}, f32[8,8]{1,0:T(8,128)S(1)}, f32[16,32,128]{2,1,0:T(8,128)S(1)}) %tuple.84, (f32[8,20,36,128]{3,2,1,0:T(8,128)S(1)}, f32[32]{0:T(128)S(1)}, ...), branch_computations={%region_0.2_spmd, %region_2.3_spmd} | conditional | flops 155859008 | bytes 44961804 | solution.py:156
  41.5 3.2 %reduce_sum.27 = f32[3,16,32,128]{3,2,1,0:T(8,128)} reduce(f32[4,3,16,32,128]{4,3,2,1,0:T(8,128)} %get-tuple-element.69, f32[]{:T(128)} %constant.79.clone), dimensions={0}, to_apply=%region_1.1 | reduce | flops 589824 | bytes 3932164 | tf_op jit(solution)/shard_map/reduce_sum | solution.py:35
  46.0 1.7 %copy.15 = f32[8,20,36,128]{3,0,2,1:T(8,128)S(1)} copy(f32[8,20,36,128]{3,2,1,0:T(8,128)S(1)} %get-tuple-element.107) | data formatting | bytes 5898240 | tf_op jit(solution)/shard_map
  47.9 6.1 %fusion.8 = f32[8,16,32,128]{3,0,2,1:T(8,128)S(1)} fusion(f32[8,16,32,128]{3,0,2,1:T(8,128)S(1)} %slice.573, f32[8,20,36,128]{3,0,2,1:T(8,128)S(1)} %copy.15, f32[16,32,128]{2,1,0:T(8,128)S(1)} %get-tuple-element.71, f32[16,32,128]{2,1,0:T(8,128)S(1)} %get-tuple-element.121, f32[16,32,128]{2,1,0:T(8,128)S(1)} %get-tuple-element.122, ...), kind=kOutput, calls=%fused_computation.10 | convolution fusion | flops 72351744 | bytes 24645632 | tf_op jit(solution)/shard_map/cond/branch_0_fun/ij,jxyz->ixyz/dot_general | solution.py:109
  57.1 3.8 %collective-permute-done.4 = f32[8,2,32,128]{3,2,1,0:T(8,128)S(1)} collective-permute-done((f32[8,2,32,128]{3,2,1,0:T(8,128)S(1)}, f32[8,2,32,128]{3,2,1,0:T(8,128)S(1)}, u32[]{:S(2)}, u32[]{:S(2)}) %collective-permute-start.4) | collective-permute-done | bytes 262176 | tf_op jit(solution)/shard_map/ppermute | solution.py:24
  60.9 3.1 %collective-permute-done.5 = f32[8,2,32,128]{3,2,1,0:T(8,128)S(1)} collective-permute-done((f32[8,2,32,128]{3,2,1,0:T(8,128)S(1)}, f32[8,2,32,128]{3,2,1,0:T(8,128)S(1)}, u32[]{:S(2)}, u32[]{:S(2)}) %collective-permute-start.5) | collective-permute-done | bytes 262176 | tf_op jit(solution)/shard_map/ppermute | solution.py:26
  65.4 2.1 %collective-permute-start.7 = (f32[8,20,2,128]{3,2,1,0:T(2,128)S(1)}, f32[8,20,2,128]{3,2,1,0:T(2,128)S(1)}, u32[]{:S(2)}, u32[]{:S(2)}) collective-permute-start(f32[8,20,2,128]{3,2,1,0:T(2,128)S(1)} %get-tuple-element.161), channel_id=1, source_target_pairs={{1,0},{2,1},{3,2},{0,3},{5,4},{6,5},{7,6},{4,7},{9,8},{10,9},{11,1... | collective-permute-start | bytes 491528 | tf_op jit(solution)/shard_map/ppermute | solution.py:26
  67.4 2.8 %collective-permute-done.6 = f32[8,20,2,128]{3,2,1,0:T(2,128)S(1)} collective-permute-done((f32[8,20,2,128]{3,2,1,0:T(2,128)S(1)}, f32[8,20,2,128]{3,2,1,0:T(2,128)S(1)}, u32[]{:S(2)}, u32[]{:S(2)}) %collective-permute-start.6) | collective-permute-done | bytes 163872 | tf_op jit(solution)/shard_map/ppermute | solution.py:24
  71.7 2.1 %maximum_multiply_fusion.1 = f32[8,20,36,128]{3,2,1,0:T(8,128)S(1)} fusion(f32[8,20,2,128]{3,2,1,0:T(2,128)S(1)} %collective-permute-done.7, f32[8,2,32,128]{3,2,1,0:T(8,128)S(1)} %collective-permute-done.5, f32[8,16,32,128]{3,2,1,0:T(8,128)} %copy-done.3, f32[8,2,32,128]{3,2,1,0:T(8,128)S(1)} %collective-permute-done.4, ...), kind=kLoop, calls=%fused_computation.187 | loop fusion | flops 3686400 | bytes 5898384 | tf_op jit(solution)/shard_map/mul | solution.py:161
  73.8 10.3 %all-gather.9.cloned.1.call-done = f32[12,16,32,128]{3,2,1,0:T(8,128)} async-done(((f32[3,16,32,128]{3,2,1,0:T(8,128)}), f32[12,16,32,128]{3,2,1,0:T(8,128)}) %all-gather.9.cloned.1.call-update) | async-done | bytes 3145744 | tf_op jit(solution)/shard_map/all_gather | solution.py:35
  84.1 12.9 %conditional.4 = (f32[8,16,32,128]{3,2,1,0:T(8,128)S(1)}) conditional(s32[]{:T(128)} %convert_element_type.41, (f32[8,20,36,128]{3,2,1,0:T(8,128)S(1)}, f32[4,3,16,32,128]{4,3,2,1,0:T(8,128)}, f32[8,8]{1,0:T(8,128)S(1)}, f32[16,32,128]{2,1,0:T(8,128)S(1)}) %tuple.86, (f32[8,20,36,128]{3,2,1,0:T(8,128)S(1)}, f32[32]{0:T(128)S(1)}, ...), branch_computations={%region_3.5_spmd, %region_5.6_spmd} | conditional | flops 155859008 | bytes 44961804 | solution.py:156
  84.2 3.2 %reduce_sum.28 = f32[3,16,32,128]{3,2,1,0:T(8,128)} reduce(f32[4,3,16,32,128]{4,3,2,1,0:T(8,128)} %get-tuple-element.77, f32[]{:T(128)} %constant.129.clone), dimensions={0}, to_apply=%region_4.4 | reduce | flops 589824 | bytes 3932164 | tf_op jit(solution)/shard_map/reduce_sum | solution.py:35
  88.6 1.7 %copy.16 = f32[8,20,36,128]{3,0,2,1:T(8,128)S(1)} copy(f32[8,20,36,128]{3,2,1,0:T(8,128)S(1)} %get-tuple-element.111) | data formatting | bytes 5898240 | tf_op jit(solution)/shard_map
  90.5 6.1 %fusion.46 = f32[8,16,32,128]{3,0,2,1:T(8,128)S(1)} fusion(f32[8,16,32,128]{3,0,2,1:T(8,128)S(1)} %slice.596, f32[8,20,36,128]{3,0,2,1:T(8,128)S(1)} %copy.16, f32[16,32,128]{2,1,0:T(8,128)S(1)} %get-tuple-element.79, f32[16,32,128]{2,1,0:T(8,128)S(1)} %get-tuple-element.134, f32[16,32,128]{2,1,0:T(8,128)S(1)} %get-tuple-element.135, ...), kind=kOutput, calls=%fused_computation.72 | convolution fusion | flops 72351744 | bytes 24645632 | tf_op jit(solution)/shard_map/cond/branch_0_fun/ij,jxyz->ixyz/dot_general | solution.py:109
  99.7 3.8 %collective-permute-done.8 = f32[8,2,32,128]{3,2,1,0:T(8,128)S(1)} collective-permute-done((f32[8,2,32,128]{3,2,1,0:T(8,128)S(1)}, f32[8,2,32,128]{3,2,1,0:T(8,128)S(1)}, u32[]{:S(2)}, u32[]{:S(2)}) %collective-permute-start.8) | collective-permute-done | bytes 262176 | tf_op jit(solution)/shard_map/ppermute | solution.py:24
  103.5 3.1 %collective-permute-done.9 = f32[8,2,32,128]{3,2,1,0:T(8,128)S(1)} collective-permute-done((f32[8,2,32,128]{3,2,1,0:T(8,128)S(1)}, f32[8,2,32,128]{3,2,1,0:T(8,128)S(1)}, u32[]{:S(2)}, u32[]{:S(2)}) %collective-permute-start.9) | collective-permute-done | bytes 262176 | tf_op jit(solution)/shard_map/ppermute | solution.py:26
  108.0 2.1 %collective-permute-start.11 = (f32[8,20,2,128]{3,2,1,0:T(2,128)S(1)}, f32[8,20,2,128]{3,2,1,0:T(2,128)S(1)}, u32[]{:S(2)}, u32[]{:S(2)}) collective-permute-start(f32[8,20,2,128]{3,2,1,0:T(2,128)S(1)} %get-tuple-element.159), channel_id=1, source_target_pairs={{1,0},{2,1},{3,2},{0,3},{5,4},{6,5},{7,6},{4,7},{9,8},{10,9},{11,1... | collective-permute-start | bytes 491528 | tf_op jit(solution)/shard_map/ppermute | solution.py:26
  110.0 2.8 %collective-permute-done.10 = f32[8,20,2,128]{3,2,1,0:T(2,128)S(1)} collective-permute-done((f32[8,20,2,128]{3,2,1,0:T(2,128)S(1)}, f32[8,20,2,128]{3,2,1,0:T(2,128)S(1)}, u32[]{:S(2)}, u32[]{:S(2)}) %collective-permute-start.10) | collective-permute-done | bytes 163872 | tf_op jit(solution)/shard_map/ppermute | solution.py:24
  114.3 2.1 %maximum_multiply_fusion.2 = f32[8,20,36,128]{3,2,1,0:T(8,128)S(1)} fusion(f32[8,20,2,128]{3,2,1,0:T(2,128)S(1)} %collective-permute-done.11, f32[8,2,32,128]{3,2,1,0:T(8,128)S(1)} %collective-permute-done.9, f32[8,16,32,128]{3,2,1,0:T(8,128)} %copy-done.4, f32[8,2,32,128]{3,2,1,0:T(8,128)S(1)} %collective-permute-done.8, ...), kind=kLoop, calls=%fused_computation.188 | loop fusion | flops 3686400 | bytes 5898384 | tf_op jit(solution)/shard_map/mul | solution.py:161
  116.4 10.4 %all-gather.11.cloned.1.call-done = f32[12,16,32,128]{3,2,1,0:T(8,128)} async-done(((f32[3,16,32,128]{3,2,1,0:T(8,128)}), f32[12,16,32,128]{3,2,1,0:T(8,128)}) %all-gather.11.cloned.1.call-update) | async-done | bytes 3145744 | tf_op jit(solution)/shard_map/all_gather | solution.py:35
  126.8 13.1 %conditional.5 = (f32[8,16,32,128]{3,2,1,0:T(8,128)S(1)}) conditional(s32[]{:T(128)} %convert_element_type.41, (f32[8,20,36,128]{3,2,1,0:T(8,128)S(1)}, f32[4,3,16,32,128]{4,3,2,1,0:T(8,128)}, f32[8,8]{1,0:T(8,128)S(1)}, f32[16,32,128]{2,1,0:T(8,128)S(1)}) %tuple.85, (f32[8,20,36,128]{3,2,1,0:T(8,128)S(1)}, f32[32]{0:T(128)S(1)}, ...), branch_computations={%region_6.8_spmd, %region_8.9_spmd} | conditional | flops 155859008 | bytes 44961804 | solution.py:156
  126.8 3.2 %reduce_sum.29 = f32[3,16,32,128]{3,2,1,0:T(8,128)} reduce(f32[4,3,16,32,128]{4,3,2,1,0:T(8,128)} %get-tuple-element.85, f32[]{:T(128)} %constant.163.clone), dimensions={0}, to_apply=%region_7.7 | reduce | flops 589824 | bytes 3932164 | tf_op jit(solution)/shard_map/reduce_sum | solution.py:35
  133.1 6.1 %fusion.84 = f32[8,16,32,128]{3,0,2,1:T(8,128)S(1)} fusion(f32[8,16,32,128]{3,0,2,1:T(8,128)S(1)} %slice.619, f32[8,20,36,128]{3,0,2,1:T(8,128)S(1)} %copy.17, f32[16,32,128]{2,1,0:T(8,128)S(1)} %get-tuple-element.87, f32[16,32,128]{2,1,0:T(8,128)S(1)} %get-tuple-element.147, f32[16,32,128]{2,1,0:T(8,128)S(1)} %get-tuple-element.148, ...), kind=kOutput, calls=%fused_computation.134 | convolution fusion | flops 72351744 | bytes 24645632 | tf_op jit(solution)/shard_map/cond/branch_0_fun/ij,jxyz->ixyz/dot_general | solution.py:109
  (60 shorter events, 25.5 us)
Async XLA Ops:
  6.5 6.6 %copy-start = (f32[3,8,8]{2,1,0:T(8,128)S(1)}, f32[3,8,8]{2,1,0:T(8,128)}, u32[]{:S(2)}) copy-start(f32[3,8,8]{2,1,0:T(8,128)} %param.11) | copy-start | bytes 2308
  6.5 35.0 %all-gather.7.cloned.1.call-start = ((), (), s32[]{:S(2)}) async-start(), calls=%async_computation | async-start | bytes 3932160 | tf_op jit(solution)/shard_map/all_gather | solution.py:35
  9.3 15.1 %copy-start.2 = (f32[8,16,32,128]{3,2,1,0:T(8,128)}, f32[8,16,32,128]{3,2,1,0:T(8,128)S(1)}, u32[]{:S(2)}) copy-start(f32[8,16,32,128]{3,2,1,0:T(8,128)S(1)} %broadcast_multiply_fusion) | copy-start | bytes 6291460
  10.4 73.8 %all-gather.9.cloned.1.call-start = ((), (), s32[]{:S(2)}) async-start(), calls=%async_computation.1 | async-start | bytes 3932160 | tf_op jit(solution)/shard_map/all_gather | solution.py:35
  10.5 8.1 %collective-permute-start = (f32[8,2,32,128]{3,2,1,0:T(8,128)S(1)}, f32[8,2,32,128]{3,2,1,0:T(8,128)S(1)}, u32[]{:S(2)}, u32[]{:S(2)}) collective-permute-start(f32[8,2,32,128]{3,2,1,0:T(8,128)S(1)} %get-tuple-element.168), channel_id=1, source_target_pairs={{0,4},{4,0},{1,5},{5,1},{2,6},{6,2},{3,7},{7,3},{8,12},{12,8},{9,1... | collective-permute-start | bytes 786440 | tf_op jit(solution)/shard_map/ppermute | solution.py:24
  12.6 11.7 %collective-permute-start.1 = (f32[8,2,32,128]{3,2,1,0:T(8,128)S(1)}, f32[8,2,32,128]{3,2,1,0:T(8,128)S(1)}, u32[]{:S(2)}, u32[]{:S(2)}) collective-permute-start(f32[8,2,32,128]{3,2,1,0:T(8,128)S(1)} %get-tuple-element.169), channel_id=1, source_target_pairs={{4,0},{0,4},{5,1},{1,5},{6,2},{2,6},{7,3},{3,7},{12,8},{8,12},{13,... | collective-permute-start | bytes 786440 | tf_op jit(solution)/shard_map/ppermute | solution.py:26
  18.6 12.4 %copy-start.6 = (f32[8,2,32,128]{3,2,1,0:T(8,128)}, f32[8,2,32,128]{3,2,1,0:T(8,128)S(1)}, u32[]{:S(2)}) copy-start(f32[8,2,32,128]{3,2,1,0:T(8,128)S(1)} %collective-permute-done) | copy-start | bytes 786436
  24.3 6.6 %copy-start.7 = (f32[8,2,32,128]{3,2,1,0:T(8,128)}, f32[8,2,32,128]{3,2,1,0:T(8,128)S(1)}, u32[]{:S(2)}) copy-start(f32[8,2,32,128]{3,2,1,0:T(8,128)S(1)} %collective-permute-done.1) | copy-start | bytes 786436
  24.4 6.5 %collective-permute-start.2 = (f32[8,20,2,128]{3,2,1,0:T(2,128)S(1)}, f32[8,20,2,128]{3,2,1,0:T(2,128)S(1)}, u32[]{:S(2)}, u32[]{:S(2)}) collective-permute-start(f32[8,20,2,128]{3,2,1,0:T(2,128)S(1)} %get-tuple-element.162), channel_id=1, source_target_pairs={{0,1},{1,2},{2,3},{3,0},{4,5},{5,6},{6,7},{7,4},{8,9},{9,10},{10,1... | collective-permute-start | bytes 491528 | tf_op jit(solution)/shard_map/ppermute | solution.py:24
  25.8 9.2 %collective-permute-start.3 = (f32[8,20,2,128]{3,2,1,0:T(2,128)S(1)}, f32[8,20,2,128]{3,2,1,0:T(2,128)}, u32[]{:S(2)}, u32[]{:S(2)}) collective-permute-start(f32[8,20,2,128]{3,2,1,0:T(2,128)S(1)} %get-tuple-element.163), channel_id=1, source_target_pairs={{1,0},{2,1},{3,2},{0,3},{5,4},{6,5},{7,6},{4,7},{9,8},{10,9},{11,1... | collective-permute-start | bytes 491528 | tf_op jit(solution)/shard_map/ppermute | solution.py:26
  28.5 13.0 %copy-start.9 = (f32[32]{0:T(128)S(1)}, f32[32]{0:T(128)}, u32[]{:S(2)}) copy-start(f32[32]{0:T(128)} %multiply_add_fusion.3) | copy-start | bytes 388
  30.9 0.7 copy-start.8
  54.4 9.7 %copy-start.3 = (f32[8,16,32,128]{3,2,1,0:T(8,128)}, f32[8,16,32,128]{3,2,1,0:T(8,128)S(1)}, u32[]{:S(2)}) copy-start(f32[8,16,32,128]{3,2,1,0:T(8,128)S(1)} %get-tuple-element.172) | copy-start | bytes 6291460
  55.5 71.3 %all-gather.11.cloned.1.call-start = ((), (), s32[]{:S(2)}) async-start(), calls=%async_computation.2 | async-start | bytes 3932160 | tf_op jit(solution)/shard_map/all_gather | solution.py:35
  55.6 5.3 %collective-permute-start.4 = (f32[8,2,32,128]{3,2,1,0:T(8,128)S(1)}, f32[8,2,32,128]{3,2,1,0:T(8,128)S(1)}, u32[]{:S(2)}, u32[]{:S(2)}) collective-permute-start(f32[8,2,32,128]{3,2,1,0:T(8,128)S(1)} %get-tuple-element.166), channel_id=1, source_target_pairs={{0,4},{4,0},{1,5},{5,1},{2,6},{6,2},{3,7},{7,3},{8,12},{12,8},{9,1... | collective-permute-start | bytes 786440 | tf_op jit(solution)/shard_map/ppermute | solution.py:24
  56.8 7.1 %collective-permute-start.5 = (f32[8,2,32,128]{3,2,1,0:T(8,128)S(1)}, f32[8,2,32,128]{3,2,1,0:T(8,128)S(1)}, u32[]{:S(2)}, u32[]{:S(2)}) collective-permute-start(f32[8,2,32,128]{3,2,1,0:T(8,128)S(1)} %get-tuple-element.167), channel_id=1, source_target_pairs={{4,0},{0,4},{5,1},{1,5},{6,2},{2,6},{7,3},{3,7},{12,8},{8,12},{13,... | collective-permute-start | bytes 786440 | tf_op jit(solution)/shard_map/ppermute | solution.py:26
  64.1 6.1 %collective-permute-start.6 = (f32[8,20,2,128]{3,2,1,0:T(2,128)S(1)}, f32[8,20,2,128]{3,2,1,0:T(2,128)S(1)}, u32[]{:S(2)}, u32[]{:S(2)}) collective-permute-start(f32[8,20,2,128]{3,2,1,0:T(2,128)S(1)} %get-tuple-element.160), channel_id=1, source_target_pairs={{0,1},{1,2},{2,3},{3,0},{4,5},{5,6},{6,7},{7,4},{8,9},{9,10},{10,1... | collective-permute-start | bytes 491528 | tf_op jit(solution)/shard_map/ppermute | solution.py:24
  65.4 6.3 %collective-permute-start.7 = (f32[8,20,2,128]{3,2,1,0:T(2,128)S(1)}, f32[8,20,2,128]{3,2,1,0:T(2,128)S(1)}, u32[]{:S(2)}, u32[]{:S(2)}) collective-permute-start(f32[8,20,2,128]{3,2,1,0:T(2,128)S(1)} %get-tuple-element.161), channel_id=1, source_target_pairs={{1,0},{2,1},{3,2},{0,3},{5,4},{6,5},{7,6},{4,7},{9,8},{10,9},{11,1... | collective-permute-start | bytes 491528 | tf_op jit(solution)/shard_map/ppermute | solution.py:26
  97.1 9.6 %copy-start.4 = (f32[8,16,32,128]{3,2,1,0:T(8,128)}, f32[8,16,32,128]{3,2,1,0:T(8,128)S(1)}, u32[]{:S(2)}) copy-start(f32[8,16,32,128]{3,2,1,0:T(8,128)S(1)} %get-tuple-element.173) | copy-start | bytes 6291460
  98.2 5.3 %collective-permute-start.8 = (f32[8,2,32,128]{3,2,1,0:T(8,128)S(1)}, f32[8,2,32,128]{3,2,1,0:T(8,128)S(1)}, u32[]{:S(2)}, u32[]{:S(2)}) collective-permute-start(f32[8,2,32,128]{3,2,1,0:T(8,128)S(1)} %get-tuple-element.164), channel_id=1, source_target_pairs={{0,4},{4,0},{1,5},{5,1},{2,6},{6,2},{3,7},{7,3},{8,12},{12,8},{9,1... | collective-permute-start | bytes 786440 | tf_op jit(solution)/shard_map/ppermute | solution.py:24
  99.4 7.1 %collective-permute-start.9 = (f32[8,2,32,128]{3,2,1,0:T(8,128)S(1)}, f32[8,2,32,128]{3,2,1,0:T(8,128)S(1)}, u32[]{:S(2)}, u32[]{:S(2)}) collective-permute-start(f32[8,2,32,128]{3,2,1,0:T(8,128)S(1)} %get-tuple-element.165), channel_id=1, source_target_pairs={{4,0},{0,4},{5,1},{1,5},{6,2},{2,6},{7,3},{3,7},{12,8},{8,12},{13,... | collective-permute-start | bytes 786440 | tf_op jit(solution)/shard_map/ppermute | solution.py:26
  106.7 6.1 %collective-permute-start.10 = (f32[8,20,2,128]{3,2,1,0:T(2,128)S(1)}, f32[8,20,2,128]{3,2,1,0:T(2,128)S(1)}, u32[]{:S(2)}, u32[]{:S(2)}) collective-permute-start(f32[8,20,2,128]{3,2,1,0:T(2,128)S(1)} %get-tuple-element.158), channel_id=1, source_target_pairs={{0,1},{1,2},{2,3},{3,0},{4,5},{5,6},{6,7},{7,4},{8,9},{9,10},{10,1... | collective-permute-start | bytes 491528 | tf_op jit(solution)/shard_map/ppermute | solution.py:24
  108.0 6.3 %collective-permute-start.11 = (f32[8,20,2,128]{3,2,1,0:T(2,128)S(1)}, f32[8,20,2,128]{3,2,1,0:T(2,128)S(1)}, u32[]{:S(2)}, u32[]{:S(2)}) collective-permute-start(f32[8,20,2,128]{3,2,1,0:T(2,128)S(1)} %get-tuple-element.159), channel_id=1, source_target_pairs={{1,0},{2,1},{3,2},{0,3},{5,4},{6,5},{7,6},{4,7},{9,8},{10,9},{11,1... | collective-permute-start | bytes 491528 | tf_op jit(solution)/shard_map/ppermute | solution.py:26
  139.9 1.3 copy-start.5
  141.2 0.7 copy-start.1
Sparse Core Ops, SparseCore 0:
  10.5 30.9 all-gather.6
  55.6 28.4 all-gather.8
  98.2 28.4 all-gather.10
